TPU v7x, 128 devices: a whole 4x4x4 slice. The times are simulated.
128 devices in a mesh: row: 16 (over y, x), col: 8 (over z, core).
Axes of the slice: x: 4, y: 4, z: 4, core: 2. Of those that a mesh axis runs over, the one named last changes fastest.
Arguments:
- panel_cols: float32 [256, 16384], P('col', 'row'), as said below
- window_cols: float32 [16384, 16384], P('col', 'row'), may hold values from -6 to 6
Outputs:
- triangle: float32 [256, 256], replicated
- top_rows: float32 [16384, 256], P(('col', 'row'))
- residual: float32 [16384, 16384], P('col', 'row')
Inputs may be any that keep to these rules, and one draw needn't show every extreme that they name: `panel_cols`: the 256 rows are linearly independent over the 1024 columns of every block of row.
All inputs are finite; a program needn't handle non-finite values.
Results may differ from a plain program's by a relative error of at most 0.000084.
Values sent between devices are 32-bit elements; how exact they have to be, the bound alone decides.
A program may use at most 64 MiB of HBM per device.

v0:
```python
import jax
import jax.numpy as jnp
from jax import lax
from jax.sharding import PartitionSpec as P

precise = lax.Precision.HIGHEST


def outer_sum(left, right):
    return lax.dot_general(
        left, right, (((1,), (1,)), ((), ())), precision=precise, preferred_element_type=jnp.float32
    )


def lower_inverse(lower_part):
    identity = jnp.eye(lower_part.shape[0], dtype=jnp.float32)
    return lax.linalg.triangular_solve(lower_part, identity, left_side=True, lower=True)


def local(panel_cols, window_cols):
    slab = window_cols.shape[0]
    whole = lax.all_gather(panel_cols, "col", axis=0, tiled=True)
    cross = outer_sum(window_cols, whole)
    gram_local = outer_sum(whole, whole)
    gram_total, cross_total = lax.psum((gram_local, cross), "row")
    lower_part = jnp.linalg.cholesky(gram_total)
    inverse = lower_inverse(lower_part)
    top_all = outer_sum(cross_total, inverse)
    share_rows = slab // lax.axis_size("row")
    top_rows = lax.dynamic_slice_in_dim(top_all, lax.axis_index("row") * share_rows, share_rows, 0)
    combined = jnp.dot(top_all, inverse, precision=precise, preferred_element_type=jnp.float32)
    residual = window_cols - jnp.dot(
        combined, whole, precision=precise, preferred_element_type=jnp.float32
    )
    return (lower_part.T, top_rows, residual)


def solution(mesh):
    return jax.shard_map(
        local,
        mesh=mesh,
        in_specs=(P("col", "row"), P("col", "row")),
        out_specs=(P(), P(("col", "row"), None), P("col", "row")),
        check_vma=False,
    )
```

profile of v0, /device:TPU:0, one launch (start us, length us, event | category | flops | bytes accessed | tf_op | source)
XLA Modules:
  0.0 238.2 jit_solution(10998402472128093950)
XLA Ops:
  7.2 0.0 all-gather.2.cloned.1.call-start
  7.2 0.7 all-gather.2.cloned.1.call-update
  7.9 0.0 all-reduce.4.cloned.1.call-start
  7.9 27.7 %all-gather.2.cloned.1.call-done = f32[256,1024]{1,0:T(8,128)} async-done(((f32[32,1024]{1,0:T(8,128)}), f32[256,1024]{1,0:T(8,128)}) %all-gather.2.cloned.1.call-update) | async-done | bytes 1048592 | tf_op jit(solution)/shard_map/all_gather | solution.py:22
  35.7 3.4 %fusion.15 = f32[256,256]{0,1:T(8,128)} fusion(f32[256,1024]{1,0:T(8,128)} %all-gather.2.cloned.1.call-done), kind=kOutput, calls=%fused_computation.38 | convolution fusion | flops 805306368 | bytes 1310720 | tf_op jit(solution)/shard_map/dot_general | solution.py:10
  39.0 10.1 %fusion.16 = f32[2048,256]{1,0:T(8,128)} fusion(f32[2048,1024]{1,0:T(8,128)} %param.3, f32[256,1024]{1,0:T(8,128)S(1)} %copy-done), kind=kOutput, calls=%fused_computation.39 | convolution fusion | flops 6442450944 | bytes 11534336 | tf_op jit(solution)/shard_map/dot_general | solution.py:10
  49.2 91.9 %all-reduce.4.cloned.1.call-done = (f32[256,256]{0,1:T(8,128)}, f32[2048,256]{1,0:T(8,128)}) async-done(((f32[256,256]{0,1:T(8,128)}, f32[2048,256]{1,0:T(8,128)}), (f32[256,256]{0,1:T(8,128)}, f32[2048,256]{1,0:T(8,128)})) %all-reduce.4.cloned.1.call-update) | async-done | bytes 2359312 | tf_op jit(solution)/shard_map/psum | solution.py:25
  141.1 1.1 copy.6
  142.2 1.0 fusion
  143.2 0.7 copy-done.3
  143.9 11.7 %cholesky.50 = f32[128,128]{1,0:T(8,128)S(1)} custom-call(f32[128,128]{1,0:T(8,128)S(1)} %cholesky.118), custom_call_target="Cholesky" | custom-call | tf_op jit(solution)/shard_map/jit(cholesky)/cholesky | solution.py:26
  155.7 10.4 %custom-call.14 = f32[1,128,128]{1,2,0:T(8,128)} custom-call(f32[1,128,128]{2,1,0:T(8,128)S(1)} %get-tuple-element.31), custom_call_target="InvertDiagBlocksLowerTriangular" | custom-call | tf_op jit(solution)/shard_map/jit(cholesky)/cholesky | solution.py:26
  166.2 1.1 constant_dynamic-update-slice_fusion
  167.2 1.7 convolution_subtract_fusion.2
  169.0 12.5 %cholesky.105 = f32[128,128]{1,0:T(8,128)S(1)} custom-call(f32[128,128]{1,0:T(8,128)} %convolution_subtract_fusion.2), custom_call_target="Cholesky" | custom-call | tf_op jit(solution)/shard_map/jit(cholesky)/cholesky | solution.py:26
  181.6 0.6 compare_reduce_fusion
  183.5 1.7 fusion.1
  185.2 1.8 copy.7
  187.0 0.1 triangular_solve.44
  187.1 5.2 %while.1 = (s32[]{:T(128)}, f32[256,256]{1,0:T(8,128)S(1)}, s32[2,2]{1,0:T(2,128)S(1)}, f32[2,128,128]{2,1,0:T(8,128)}, s32[]{:T(128)}) while((s32[]{:T(128)}, f32[256,256]{1,0:T(8,128)S(1)}, s32[2,2]{1,0:T(2,128)S(1)}, f32[2,128,128]{2,1,0:T(8,128)}, s32[]{:T(128)}) %tuple.29), condition=%wide.while_cond, body=%wide.while_body.sunk | while | flops 2 | bytes 132205 | solution.py:17
  187.1 0.6 fusion.30
  187.7 2.0 bitcast_dynamic-update-slice_fusion.2
  189.7 0.6 fusion.30
  190.2 2.0 bitcast_dynamic-update-slice_fusion.2
  192.2 21.1 %custom-call.15 = f32[2,128,128]{1,2,0:T(8,128)} custom-call(f32[2,128,128]{2,1,0:T(8,128)} %get-tuple-element.10), custom_call_target="InvertDiagBlocksLowerTriangular" | custom-call | tf_op jit(solution)/shard_map/triangular_solve | solution.py:17
  213.3 1.1 fusion.5
  214.5 0.3 convolution_subtract_fusion.1
  214.7 1.2 fusion.8
  215.9 1.9 fusion.4
  217.8 1.9 fusion.3
  219.7 0.7 constant_dynamic-slice_fusion.1
  220.4 11.0 %convolution_subtract_fusion = f32[2048,1024]{1,0:T(8,128)} fusion(f32[2048,1024]{1,0:T(8,128)} %param.3, f32[2048,256]{1,0:T(8,128)S(1)} %fusion.3, f32[256,1024]{1,0:T(8,128)S(1)} %copy-done), kind=kOutput, calls=%fused_computation.2 | convolution fusion | flops 6444548096 | bytes 19922944 | tf_op jit(solution)/shard_map/dot_general | solution.py:32
  (17 shorter events, 0.2 us)
Async XLA Ops:
  7.2 28.5 %all-gather.2.cloned.1.call-start = ((), (), s32[]{:S(2)}) async-start(), calls=%async_computation | async-start | bytes 1179648 | tf_op jit(solution)/shard_map/all_gather | solution.py:22
  7.9 133.2 %all-reduce.4.cloned.1.call-start = ((), (), s32[]{:S(2)}) async-start(), calls=%async_computation.1 | async-start | bytes 4718592 | tf_op jit(solution)/shard_map/psum | solution.py:25
  35.7 3.4 %copy-start = (f32[256,1024]{1,0:T(8,128)S(1)}, f32[256,1024]{1,0:T(8,128)}, u32[]{:S(2)}) copy-start(f32[256,1024]{1,0:T(8,128)} %all-gather.2.cloned.1.call-done) | copy-start | bytes 3145732
  143.2 0.7 copy-start.3
  155.6 60.2 %copy-start.1 = (f32[2048,256]{1,0:T(8,128)S(1)}, f32[2048,256]{1,0:T(8,128)}, u32[]{:S(2)}) copy-start(f32[2048,256]{1,0:T(8,128)} %get-tuple-element.23) | copy-start | bytes 6291460
  181.6 1.9 copy-start.2
Sparse Core Ops, SparseCore 0:
  9.7 25.9 all-gather.1
  49.3 91.8 all-reduce.3
where the time goes:
time: 239 us; the launch traced here: 238 us
  waiting for transfers between devices  120 us (50%)
  other arithmetic  59.2 us (25%)
  matrix products  33.6 us (14%)
  between operations  15.5 us (6%)
  local copies, waits for them, and re-layouts  9.51 us (4%)
    psum x1, waiting for transfers between devices, local(): gram_total, cross_total = lax.psum((gram_local, cross), 'row')  91.9 us
    another operation x6, other arithmetic, local(): lower_part = jnp.linalg.cholesky(gram_total)  35.4 us
    all_gather x1, waiting for transfers between devices, local(): whole = lax.all_gather(panel_cols, 'col', axis=0, tiled=True)  27.7 us
    another operation x3, other arithmetic, lower_inverse(): lax.linalg.triangular_solve(lower_part, identity, left_side=True, lower=T...  22.8 us
    dot_general x3, matrix products, outer_sum(): lax.dot_general(left, right, (((1,), (1,)), ((), ())), precision=precise,...  15.4 us
    dot_general x1, matrix products, local(): jnp.dot(combined, whole, precision=precise, preferred_element_type=jnp.fl...  11 us
    another operation x6, local copies, waits for them, and re-layouts  5.17 us
  transfers between devices with their start and end apart: 2, of which 2 were waited for; matrix products, arithmetic and copies ran while one was open for 0% of the time, Pallas kernels for 0%

commit v1 on v0

--- a/solution.py
+++ b/solution.py
@@ -19,7 +19,8 @@
 
 def local(panel_cols, window_cols):
     slab = window_cols.shape[0]
-    whole = lax.all_gather(panel_cols, "col", axis=0, tiled=True)
+    outgoing = jnp.stack([panel_cols] * lax.axis_size("col"))
+    whole = jnp.concatenate(lax.all_to_all(outgoing, "col", 0, 0), axis=0)
     cross = outer_sum(window_cols, whole)
     gram_local = outer_sum(whole, whole)
     gram_total, cross_total = lax.psum((gram_local, cross), "row")

time: 239 us -> 231 us (0.967)
  waiting for transfers between devices: 120 us -> 91.6 us
  blocking collectives: 0 us -> 21.2 us
    all_gather x1 -> x0, waiting for transfers between devices: 27.7 us -> none  [local(): whole = lax.all_gather(panel_cols, 'col', axis=0, tiled=True)]
    all_to_all x0 -> x1, blocking collectives: none -> 21.2 us  [local(): whole = jnp.concatenate(lax.all_to_all(outgoing, 'col', 0, 0), axis=0)]
    another operation x6 -> x7, local copies, waits for them, and re-layouts: 5.17 us -> 6.15 us
  transfers between devices with their start and end apart: 2 -> 1, of which waited for: 2 -> 1; matrix products, arithmetic and copies ran while one was open for 0% -> 0% of each run, Pallas kernels for 0% -> 0%
where the time goes in v1:
time: 231 us; the launch traced here: 230 us
  waiting for transfers between devices  91.6 us (40%)
  other arithmetic  59.3 us (26%)
  matrix products  31.9 us (14%)
  blocking collectives  21.2 us (9%)
  between operations  15.4 us (7%)
  local copies, waits for them, and re-layouts  10.5 us (5%)
    psum x1, waiting for transfers between devices, local(): gram_total, cross_total = lax.psum((gram_local, cross), 'row')  91.6 us
    another operation x6, other arithmetic, local(): lower_part = jnp.linalg.cholesky(gram_total)  35.4 us
    another operation x3, other arithmetic, lower_inverse(): lax.linalg.triangular_solve(lower_part, identity, left_side=True, lower=T...  22.8 us
    all_to_all x1, blocking collectives, local(): whole = jnp.concatenate(lax.all_to_all(outgoing, 'col', 0, 0), axis=0)  21.2 us
    dot_general x3, matrix products, outer_sum(): lax.dot_general(left, right, (((1,), (1,)), ((), ())), precision=precise,...  13.7 us
    dot_general x1, matrix products, local(): jnp.dot(combined, whole, precision=precise, preferred_element_type=jnp.fl...  11 us
    another operation x6, local copies, waits for them, and re-layouts  5.14 us
  transfers between devices with their start and end apart: 1, of which 1 were waited for; matrix products, arithmetic and copies ran while one was open for 0% of the time, Pallas kernels for 0%

profile of v1, /device:TPU:0, one launch (start us, length us, event | category | flops | bytes accessed | tf_op | source)
XLA Modules:
  0.0 230.0 jit_solution(1581162378213735315)
XLA Ops:
  7.2 0.0 all-reduce.4.cloned.1.call-start
  7.2 1.0 stack.2
  8.2 21.2 %all_to_all.5 = f32[8,32,1024]{2,1,0:T(8,128)S(1)} all-to-all(f32[8,32,1024]{2,1,0:T(8,128)S(1)} %stack.2), channel_id=1, replica_groups=mesh['row'=16,'col'=8] {'col'}, dimensions={0} | all-to-all | bytes 2097152 | tf_op jit(solution)/shard_map/all_to_all | solution.py:23
  29.4 1.7 fusion.15
  31.2 10.1 %fusion.16 = f32[2048,256]{1,0:T(8,128)} fusion(f32[2048,1024]{1,0:T(8,128)} %param.3, f32[256,1024]{1,0:T(8,128)S(1)} %bitcast.43), kind=kOutput, calls=%fused_computation.39 | convolution fusion | flops 6442450944 | bytes 11534336 | tf_op jit(solution)/shard_map/dot_general | solution.py:10
  41.2 0.0 all-reduce.4.cloned.1.call-update
  41.3 91.6 %all-reduce.4.cloned.1.call-done = (f32[256,256]{0,1:T(8,128)}, f32[2048,256]{1,0:T(8,128)}) async-done(((f32[256,256]{0,1:T(8,128)}, f32[2048,256]{1,0:T(8,128)}), (f32[256,256]{0,1:T(8,128)}, f32[2048,256]{1,0:T(8,128)})) %all-reduce.4.cloned.1.call-update) | async-done | bytes 2359312 | tf_op jit(solution)/shard_map/psum | solution.py:26
  132.9 1.1 copy.6
  134.0 1.0 fusion
  135.0 0.7 copy-done.2
  135.7 11.7 %cholesky.50 = f32[128,128]{1,0:T(8,128)S(1)} custom-call(f32[128,128]{1,0:T(8,128)S(1)} %cholesky.118), custom_call_target="Cholesky" | custom-call | tf_op jit(solution)/shard_map/jit(cholesky)/cholesky | solution.py:27
  147.4 10.4 %custom-call.14 = f32[1,128,128]{1,2,0:T(8,128)} custom-call(f32[1,128,128]{2,1,0:T(8,128)S(1)} %get-tuple-element.31), custom_call_target="InvertDiagBlocksLowerTriangular" | custom-call | tf_op jit(solution)/shard_map/jit(cholesky)/cholesky | solution.py:27
  157.9 1.1 constant_dynamic-update-slice_fusion
  159.0 1.7 convolution_subtract_fusion.2
  160.7 12.5 %cholesky.105 = f32[128,128]{1,0:T(8,128)S(1)} custom-call(f32[128,128]{1,0:T(8,128)} %convolution_subtract_fusion.2), custom_call_target="Cholesky" | custom-call | tf_op jit(solution)/shard_map/jit(cholesky)/cholesky | solution.py:27
  173.3 0.7 compare_reduce_fusion
  175.3 1.7 fusion.1
  177.0 1.8 copy.7
  178.8 0.1 triangular_solve.44
  178.8 5.1 %while.1 = (s32[]{:T(128)}, f32[256,256]{1,0:T(8,128)S(1)}, s32[2,2]{1,0:T(2,128)S(1)}, f32[2,128,128]{2,1,0:T(8,128)}, s32[]{:T(128)}) while((s32[]{:T(128)}, f32[256,256]{1,0:T(8,128)S(1)}, s32[2,2]{1,0:T(2,128)S(1)}, f32[2,128,128]{2,1,0:T(8,128)}, s32[]{:T(128)}) %tuple.29), condition=%wide.while_cond, body=%wide.while_body.sunk | while | flops 2 | bytes 132205 | solution.py:17
  178.8 0.6 fusion.30
  179.4 2.0 bitcast_dynamic-update-slice_fusion.2
  181.4 0.6 fusion.30
  182.0 2.0 bitcast_dynamic-update-slice_fusion.2
  184.0 21.1 %custom-call.15 = f32[2,128,128]{1,2,0:T(8,128)} custom-call(f32[2,128,128]{2,1,0:T(8,128)} %get-tuple-element.10), custom_call_target="InvertDiagBlocksLowerTriangular" | custom-call | tf_op jit(solution)/shard_map/triangular_solve | solution.py:17
  205.1 1.1 fusion.5
  206.2 0.3 convolution_subtract_fusion.1
  206.5 1.1 fusion.8
  207.6 1.9 fusion.4
  209.6 1.9 fusion.3
  211.5 0.7 constant_dynamic-slice_fusion.1
  212.1 11.0 %convolution_subtract_fusion = f32[2048,1024]{1,0:T(8,128)} fusion(f32[2048,1024]{1,0:T(8,128)} %param.3, f32[2048,256]{1,0:T(8,128)S(1)} %fusion.3, f32[256,1024]{1,0:T(8,128)S(1)} %bitcast.44), kind=kOutput, calls=%fused_computation.2 | convolution fusion | flops 6444548096 | bytes 19922944 | tf_op jit(solution)/shard_map/dot_general | solution.py:33
  (14 shorter events, 0.2 us)
Async XLA Ops:
  7.2 125.7 %all-reduce.4.cloned.1.call-start = ((), (), s32[]{:S(2)}) async-start(), calls=%async_computation.1 | async-start | bytes 4718592 | tf_op jit(solution)/shard_map/psum | solution.py:26
  135.0 0.7 copy-start.2
  147.4 60.2 %copy-start = (f32[2048,256]{1,0:T(8,128)S(1)}, f32[2048,256]{1,0:T(8,128)}, u32[]{:S(2)}) copy-start(f32[2048,256]{1,0:T(8,128)} %get-tuple-element.23) | copy-start | bytes 6291460
  173.3 1.9 copy-start.1
Sparse Core Ops, SparseCore 0:
  41.4 91.4 all-reduce.3
